TPU v7x, 128 devices: a whole 4x4x4 slice. The times are simulated.
128 devices in a mesh: tm: 32 (over z, y, core), rows: 4 (over x).
Axes of the slice: x: 4, y: 4, z: 4, core: 2. Of those that a mesh axis runs over, the one named last changes fastest.
Arguments:
- covars: bfloat16 [524288, 128], P(('tm', 'rows')), may hold values from -5 to 5
- strata: int32 [524288], P(('tm', 'rows')), may hold values from 0 to 511
- centers: int32 [524288], P(('tm', 'rows')), may hold values from 0 to 2047
- events: int32 [524288], P(('tm', 'rows')), may hold values 0 or 1
- counts: int32 [128], P(('tm', 'rows')), may hold values from 1024 to 4096, as said below
- beta: float32 [128], replicated, may hold values from -0.4 to 0.4
- frailty: float32 [2048], replicated, may hold values from -3 to 3
Outputs:
- score: float32 [128], replicated
- info: float32 [128, 128], replicated
- center_score: float32 [2048], P(('tm', 'rows'))
- center_info: float32 [2048], P(('tm', 'rows'))
- center_cross: float32 [2048, 128], P(('tm', 'rows'))
Inputs may be any that keep to these rules, and one draw needn't show every extreme that they name: `counts`: each shard's live records come first; some shard is full.
All inputs are finite; a program needn't handle non-finite values. No bound on the sum of `events` on one device may be relied on, other than what follows from the above.
Results may differ from a plain program's by a relative error of at most 0.00067.
Values sent between devices are 32-bit elements; how exact they have to be, the bound alone decides.
No kernel may reach another device: no remote copies, remote signals or barrier semaphores. Data moves between devices by JAX's collectives and lax.ppermute only.
A program may use at most 64 MiB of HBM per device.

v0:
```python
import math
import jax
import jax.numpy as jnp
from jax import lax
from jax.sharding import PartitionSpec as P

STRATA = 512
CENTERS_DEV = 16


def prefix(value, axis, join, neutral, backward):
    count, mine = (lax.axis_size(axis), lax.axis_index(axis))
    pieces = jax.tree.map(lambda part: lax.all_gather(part, axis), value)
    if backward:
        pieces = jax.tree.map(lambda part: part[::-1], pieces)
        mine = count - 1 - mine
    so_far = jax.tree.map(
        lambda part, zero: jnp.full_like(part, 0) + jnp.asarray(zero, part.dtype), value, neutral
    )

    def lap(position, so_far):
        longer = join(so_far, jax.tree.map(lambda part: part[position], pieces))
        return jax.tree.map(lambda new, old: jnp.where(position < mine, new, old), longer, so_far)

    return lax.fori_loop(0, count - 1, lap, so_far)


def add_pairs(earlier, later):
    return (earlier[0] + later[0], earlier[1] + later[1])


def add_single(earlier, later):
    return earlier + later


def block_suffix(group_ids, weights, weighted, groups):
    record_count = group_ids.shape[0]
    block_size = min(512, record_count)
    blocks = record_count // block_size
    positions = jnp.arange(block_size)
    upper = positions[None, :] >= positions[:, None]
    labels = jnp.arange(groups)
    contract = (((0,), (0,)), ((), ()))

    def advance(carry, item):
        carry_zero, carry_one = carry
        block_ids, block_weights, block_rows = item
        shared = (block_ids[:, None] == block_ids[None, :]) & upper
        local_one = jnp.dot(
            shared.astype(jnp.bfloat16), block_rows, preferred_element_type=jnp.float32
        )
        local_zero = jnp.dot(
            shared.astype(jnp.float32), block_weights, precision=lax.Precision.HIGHEST
        )
        result = (local_zero + carry_zero[block_ids], local_one + carry_one[block_ids])
        member = block_ids[:, None] == labels[None, :]
        carry_one = carry_one + lax.dot_general(
            member.astype(jnp.bfloat16), block_rows, contract, preferred_element_type=jnp.float32
        )
        carry_zero = carry_zero + jnp.dot(
            block_weights, member.astype(jnp.float32), precision=lax.Precision.HIGHEST
        )
        return ((carry_zero, carry_one), result)

    init = (jnp.zeros((groups,), jnp.float32), jnp.zeros((groups, weighted.shape[1]), jnp.float32))
    items = (
        group_ids.reshape(blocks, block_size),
        weights.reshape(blocks, block_size),
        weighted.reshape(blocks, block_size, weighted.shape[1]),
    )
    totals, outputs = lax.scan(advance, init, items, reverse=True)
    return (
        outputs[0].reshape(record_count),
        outputs[1].reshape(record_count, weighted.shape[1]),
        totals,
    )


def block_prefix(group_ids, increments, groups):
    record_count = group_ids.shape[0]
    block_size = min(512, record_count)
    blocks = record_count // block_size
    positions = jnp.arange(block_size)
    lower = positions[None, :] <= positions[:, None]
    labels = jnp.arange(groups)

    def advance(carry, item):
        block_ids, block_incr = item
        shared = ((block_ids[:, None] == block_ids[None, :]) & lower).astype(jnp.float32)
        result = jnp.dot(shared, block_incr, precision=lax.Precision.HIGHEST) + carry[block_ids]
        member = (block_ids[:, None] == labels[None, :]).astype(jnp.float32)
        return (carry + jnp.dot(block_incr, member, precision=lax.Precision.HIGHEST), result)

    totals, outputs = lax.scan(
        advance,
        jnp.zeros((groups,), jnp.float32),
        (group_ids.reshape(blocks, block_size), increments.reshape(blocks, block_size)),
    )
    return (outputs.reshape(record_count), totals)


def later_moments(totals):
    empty = (jnp.zeros_like(totals[0]), jnp.zeros_like(totals[1]))
    shard_zero, shard_one = lax.psum((totals[0], totals[1]), "rows")
    outer = prefix((shard_zero, shard_one), "tm", add_pairs, empty, True)
    inner = prefix((totals[0], totals[1]), "rows", add_pairs, empty, True)
    return add_pairs(outer, inner)


def earlier_hazard(totals):
    empty = jnp.zeros_like(totals)
    shard_sum = lax.psum(totals, "rows")
    outer = prefix(shard_sum, "tm", add_single, empty, False)
    inner = prefix(totals, "rows", add_single, empty, False)
    return outer + inner


def body(covars, strata, centers, events, counts, beta, frailty):
    record_count = covars.shape[0]
    width = covars.shape[1]
    contract = (((0,), (0,)), ((), ()))
    live = jnp.arange(record_count) < counts[0]
    eta = (
        jnp.dot(covars, beta, precision=lax.Precision.HIGHEST, preferred_element_type=jnp.float32)
        + frailty[centers]
    )
    weights = jnp.where(live, jnp.exp(eta), 0.0)
    weighted = (weights[:, None] * covars.astype(jnp.float32)).astype(jnp.bfloat16)
    suffix_zero, suffix_one, totals = block_suffix(strata, weights, weighted, STRATA)
    later_zero, later_one = later_moments(totals)
    suffix_zero = suffix_zero + later_zero[strata]
    suffix_one = suffix_one + later_one[strata]
    flags = jnp.where(live, events, 0).astype(jnp.float32)
    safe_zero = jnp.where(flags > 0, suffix_zero, 1.0)
    increments = jnp.where(flags > 0, flags / safe_zero, 0.0)
    local_hazard, hazard_totals = block_prefix(strata, increments, STRATA)
    hazard = local_hazard + earlier_hazard(hazard_totals)[strata]
    exposure = weights * hazard
    mean_rows = jnp.where(flags[:, None] > 0, suffix_one / safe_zero[:, None], 0.0)
    mean_low = mean_rows.astype(jnp.bfloat16)
    loaded = (exposure[:, None] * covars.astype(jnp.float32)).astype(jnp.bfloat16)
    gradient = jnp.dot(
        flags.astype(jnp.bfloat16), covars, preferred_element_type=jnp.float32
    ) - jnp.sum(mean_rows, axis=0)
    curvature = lax.dot_general(
        covars, loaded, contract, preferred_element_type=jnp.float32
    ) - lax.dot_general(mean_low, mean_low, contract, preferred_element_type=jnp.float32)
    gradient, curvature = lax.psum((gradient, curvature), ("tm", "rows"))
    devices = lax.axis_size("tm") * lax.axis_size("rows")
    total = record_count * devices
    score = gradient / math.sqrt(total)
    info = curvature / total
    center_total = CENTERS_DEV * devices
    pair = jnp.stack(
        [
            jax.ops.segment_sum(flags - exposure, centers, num_segments=center_total),
            jax.ops.segment_sum(exposure, centers, num_segments=center_total),
        ]
    )
    block_size = min(2048, record_count)
    blocks = record_count // block_size
    labels = jnp.arange(center_total)

    def collect(accum, item):
        block_ids, block_rows = item
        member = (block_ids[:, None] == labels[None, :]).astype(jnp.bfloat16)
        return (
            accum
            + lax.dot_general(member, block_rows, contract, preferred_element_type=jnp.float32),
            None,
        )

    cross, unused_out = lax.scan(
        collect,
        jnp.zeros((center_total, width), jnp.float32),
        (centers.reshape(blocks, block_size), loaded.reshape(blocks, block_size, width)),
    )
    cross_mine, pair_mine = (
        lax.psum_scatter(cross, ("tm", "rows"), scatter_dimension=0, tiled=True),
        lax.psum_scatter(pair, ("tm", "rows"), scatter_dimension=1, tiled=True),
    )
    load = record_count // CENTERS_DEV
    root = math.sqrt(load)
    frailty_mine = lax.dynamic_slice_in_dim(
        frailty, lax.axis_index(("tm", "rows")) * CENTERS_DEV, CENTERS_DEV
    )
    center_score = pair_mine[0] / root - 0.5 * frailty_mine
    center_info = pair_mine[1] / load + 0.5
    center_cross = cross_mine / root
    return (score, info, center_score, center_info, center_cross)


def solution(mesh):
    in_specs = (
        P(("tm", "rows"), None),
        P(("tm", "rows")),
        P(("tm", "rows")),
        P(("tm", "rows")),
        P(("tm", "rows")),
        P(),
        P(),
    )
    out_specs = (P(), P(), P(("tm", "rows")), P(("tm", "rows")), P(("tm", "rows"), None))
    return jax.shard_map(body, mesh=mesh, in_specs=in_specs, out_specs=out_specs, check_vma=False)
```

profile of v0, /device:TPU:0, one launch (start us, length us, event | category | flops | bytes accessed | tf_op | source)
XLA Modules:
  0.0 1883.2 jit_solution(13553118793809692957)
XLA Ops:
  8.6 23.0 %gather_fusion.3 = f32[4096]{0:T(1024)S(1)} fusion(f32[2048]{0:T(1024)S(1)} %copy-done.1, s32[4096]{0:T(1024)S(1)} %fusion.55), kind=kCustom, calls=%fused_computation.3 | custom fusion | bytes 49152 | tf_op jit(solution)/shard_map/gather | solution.py:125
  34.9 58.8 %while.105 = (s32[]{:T(128)}, f32[512]{0:T(512)S(1)}, f32[512,128]{1,0:T(8,128)S(1)}, f32[8,512]{1,0:T(8,128)S(1)}, f32[8,512,128]{2,1,0:T(8,128)}, /*index=5*/f...) while((s32[]{:T(128)}, f32[512]{0:T(512)S(1)}, ...), condition=%wide.region_1.2_spmd.clone, body=%wide.region_0.1_spmd.clone.sunk | while | flops 142807040 | bytes 2419864 | solution.py:71
  35.4 3.5 gather_fusion
  64.9 3.5 gather_fusion
  94.5 26.7 %all-gather.12.cloned.1.call-done = f32[2048,128]{1,0:T(8,128)} async-done(((f32[512,128]{1,0:T(8,128)}), f32[2048,128]{1,0:T(8,128)}) %all-gather.12.cloned.1.call-update) | async-done | bytes 1048592 | tf_op jit(solution)/shard_map/all_gather | solution.py:13
  122.0 44.5 %all-reduce.3.cloned.1.call-done = f32[1,512,128]{2,1,0:T(8,128)} async-done(((f32[1,512,128]{2,1,0:T(8,128)}), f32[1,512,128]{2,1,0:T(8,128)}) %all-reduce.3.cloned.1.call-update) | async-done | bytes 262160 | tf_op jit(solution)/shard_map/psum | solution.py:104
  166.6 9.3 psum.35
  176.0 24.5 %all-gather.3 = f32[32,1,512]{2,1,0:T(1,128)S(1)} all-gather(f32[1,1,512]{2,1,0:T(1,128)S(1)} %bitcast.202), channel_id=1, replica_groups=mesh['tm'=32,'rows'=4] {'tm'}, dimensions={0}, use_global_device_ids=true | all-gather | bytes 67584 | tf_op jit(solution)/shard_map/all_gather | solution.py:13
  200.5 10.4 all-gather.4
  212.9 9.2 all-gather.10.cloned.1.call-done
  222.1 7.5 rev.13
  229.7 33.7 %while.106 = (s32[]{:T(128)}, f32[512]{0:T(512)S(1)}, f32[512,128]{1,0:T(8,128)S(1)}, s32[]{:T(128)}, f32[32,512]{1,0:T(8,128)S(1)}, /*index=5*/f32[32,512,128]{2,1,0:T(8,128)}, s32[]{:T(128)}, s32[]{:T(128)}) while((s32[]{:T(128)}, f32[512]{0:T(512)S(1)}, f32[512,128]{1,0:T(8,128)S(1)}, s32[]{:T(128)}, f32[32,512]{1,0:T(8,128)S(1)}, ...), condition=%wide.region_5.6_spmd.clone, body=%wide.region_4.5_spmd.clone.sunk | while | flops 198148 | bytes 796787 | solution.py:25
  263.4 25.9 %gather_fusion.5 = f32[4096]{0:T(1024)S(1)} fusion(f32[512]{0:T(512)S(1)} %add.293, s32[4096]{0:T(1024)S(1)} %fusion.56), kind=kCustom, calls=%fused_computation.5 | custom fusion | bytes 49152 | tf_op jit(solution)/shard_map/gather | solution.py:131
  289.4 37.0 %while.108 = (s32[]{:T(128)}, f32[512]{0:T(512)S(1)}, f32[8,512]{1,0:T(8,128)S(1)}, f32[8,512]{1,0:T(8,128)S(1)}, s32[8,512]{1,0:T(8,128)S(1)}, /*index=5*/s32[]{:T(128)}, s32[]{:T(128)}) while((s32[]{:T(128)}, f32[512]{0:T(512)S(1)}, f32[8,512]{1,0:T(8,128)S(1)}, f32[8,512]{1,0:T(8,128)S(1)}, s32[8,512]{1,0:T(8,128)S(1)}, ...), condition=%wide.region_11.12_spmd.clone, body=%wide.region_10.11_spmd.clone.sunk | while | flops 7344131 | bytes 51303 | solution.py:94
  290.0 3.5 gather_fusion.2
  303.9 3.5 gather_fusion.2
  317.8 3.5 gather_fusion.2
  326.5 10.4 psum.38
  336.9 23.9 %all-gather.5 = f32[32,1,512]{2,1,0:T(1,128)S(1)} all-gather(f32[1,1,512]{2,1,0:T(1,128)S(1)} %bitcast.203), channel_id=1, replica_groups=mesh['tm'=32,'rows'=4] {'tm'}, dimensions={0}, use_global_device_ids=true | all-gather | bytes 67584 | tf_op jit(solution)/shard_map/all_gather | solution.py:13
  362.5 10.4 all-gather.6
  373.1 25.9 %gather_fusion.6 = f32[4096]{0:T(1024)S(1)} fusion(f32[512]{0:T(512)S(1)} %add.295, s32[4096]{0:T(1024)S(1)} %fusion.56), kind=kCustom, calls=%fused_computation.6 | custom fusion | bytes 49152 | tf_op jit(solution)/shard_map/gather | solution.py:137
  401.7 22.1 %scatter_custom_fusion.1 = f32[2048]{0:T(1024)S(1)} fusion(s32[4096]{0:T(1024)S(1)} %copy-done.7, f32[4096]{0:T(1024)S(1)} %get-tuple-element.902, f32[]{:T(128)} %constant.197.clone.1), kind=kCustom, calls=%fused_computation.112 | custom fusion | flops 4096 | bytes 8196 | tf_op jit(solution)/shard_map/scatter-add | solution.py:157
  423.8 14.2 gather_fusion.4
  438.0 7.1 fusion.52
  445.4 22.1 %scatter_custom_fusion = f32[2048]{0:T(1024)S(1)} fusion(s32[4096]{0:T(1024)S(1)} %copy-done.7, f32[4096]{0:T(1024)S(1)} %get-tuple-element.901, f32[]{:T(128)} %constant.197.clone.1), kind=kCustom, calls=%fused_computation.114 | custom fusion | flops 4096 | bytes 8196 | tf_op jit(solution)/shard_map/scatter-add | solution.py:156
  468.9 14.2 while.111
  469.0 7.0 fusion.107
  476.0 7.2 fusion.107
  486.7 62.7 %psum.37 = f32[128]{0:T(128)S(1)} all-reduce(f32[128]{0:T(128)S(1)} %fusion.53), channel_id=1, replica_groups=mesh['tm'=32,'rows'=4] {'tm','rows'}, use_global_device_ids=true, to_apply=%region_9.10 | all-reduce | flops 128 | bytes 1024 | tf_op jit(solution)/shard_map/psum | solution.py:148
  549.9 30.7 %all-reduce.5.cloned.1.call-done = f32[128,128]{0,1:T(8,128)} async-done(((f32[128,128]{0,1:T(8,128)}), f32[128,128]{0,1:T(8,128)}) %all-reduce.5.cloned.1.call-update) | async-done | bytes 65552 | tf_op jit(solution)/shard_map/psum | solution.py:148
  582.2 648.3 %reduce-scatter.7.cloned.1.call-done = f32[16,2]{1,0:T(8,128)} async-done(((f32[2048,2]{1,0:T(8,128)}), f32[16,2]{1,0:T(8,128)}) %reduce-scatter.7.cloned.1.call-update) | async-done | bytes 144
  1232.6 642.5 %reduce-scatter.5.cloned.1.call-done = f32[16,128]{1,0:T(8,128)} async-done(((f32[2048,128]{1,0:T(8,128)}), f32[16,128]{1,0:T(8,128)}) %reduce-scatter.5.cloned.1.call-update) | async-done | bytes 8208 | tf_op jit(solution)/shard_map/reduce_scatter | solution.py:179
  (412 shorter events, 133.8 us)
Async XLA Ops:
  7.2 24.5 %copy-start = (f32[128]{0:T(128)S(1)}, f32[128]{0:T(128)}, u32[]{:S(2)}) copy-start(f32[128]{0:T(128)} %param.26) | copy-start | bytes 1540
  7.2 1.4 copy-start.1
  7.2 114.0 %all-gather.12.cloned.1.call-start = ((), (), s32[]{:S(2)}) async-start(), calls=%async_computation.6 | async-start | bytes 1310720 | tf_op jit(solution)/shard_map/all_gather | solution.py:13
  8.6 23.1 %copy-start.2 = (bf16[4096,128]{1,0:T(8,128)(2,1)S(1)}, bf16[4096,128]{1,0:T(8,128)(2,1)}, u32[]{:S(2)}) copy-start(bf16[4096,128]{1,0:T(8,128)(2,1)} %param.21) | copy-start | bytes 3145732
  31.7 1.7 copy-start.6
  34.9 131.7 %copy-start.7 = (s32[4096]{0:T(1024)S(1)}, s32[4096]{0:T(1024)}, u32[]{:S(2)}) copy-start(s32[4096]{0:T(1024)} %param.23) | copy-start | bytes 49156
  93.7 0.7 copy-start.3
  121.2 45.3 %all-reduce.3.cloned.1.call-start = ((), (), s32[]{:S(2)}) async-start(), calls=%async_computation.2 | async-start | bytes 524288 | tf_op jit(solution)/shard_map/psum | solution.py:104
  121.9 100.2 %all-gather.10.cloned.1.call-start = ((), (), s32[]{:S(2)}) async-start(), calls=%async_computation.3 | async-start | bytes 8650752 | tf_op jit(solution)/shard_map/all_gather | solution.py:13
  166.5 414.2 %all-reduce.5.cloned.1.call-start = ((), (), s32[]{:S(2)}) async-start(), calls=%async_computation.4 | async-start | bytes 131072 | tf_op jit(solution)/shard_map/psum | solution.py:148
  263.4 26.0 %copy-start.5 = (s32[4096]{0:T(1024)S(1)}, s32[4096]{0:T(1024)}, u32[]{:S(2)}) copy-start(s32[4096]{0:T(1024)} %param.24) | copy-start | bytes 49156
  445.2 785.3 %reduce-scatter.7.cloned.1.call-start = ((), (), s32[]{:S(2)}) async-start(), calls=%async_computation.7 | async-start | bytes 1056768
  468.9 1406.2 %reduce-scatter.5.cloned.1.call-start = ((), (), s32[]{:S(2)}) async-start(), calls=%async_computation.5 | async-start | bytes 1056768 | tf_op jit(solution)/shard_map/reduce_scatter | solution.py:179
  468.9 14.3 copy-start.4
Sparse Core Ops, SparseCore 0:
  94.6 26.5 all-gather.11
  124.3 42.1 all-reduce.2
  168.7 53.3 all-gather.9
  445.3 135.3 all-reduce.4
  582.8 647.6 reduce-scatter.6
  1232.7 642.3 reduce-scatter.4
where the time goes:
time: 1880 us
  waiting for transfers between devices  1400 us (74%)
  local copies, waits for them, and re-layouts  170 us (9%)
  blocking collectives  152 us (8%)
  other arithmetic  88.2 us (5%)
  matrix products  52 us (3%)
    unnamed x7, waiting for transfers between devices  649 us
    reduce_scatter x1, waiting for transfers between devices, body(): lax.psum_scatter(cross, ('tm', 'rows'), scatter_dimension=0, tiled=True)  642 us
    all_gather x4, blocking collectives, prefix(): pieces = jax.tree.map(lambda part: lax.all_gather(part, axis), value)  69.2 us
    psum x1, blocking collectives, body(): gradient, curvature = lax.psum((gradient, curvature), ('tm', 'rows'))  62.7 us
    psum x1, waiting for transfers between devices, later_moments(): shard_zero, shard_one = lax.psum((totals[0], totals[1]), 'rows')  44.5 us
  transfers between devices with their start and end apart: 6, of which 6 were waited for; matrix products, arithmetic and copies ran while one was open for 3% of the time, Pallas kernels for 0%

commit v1 on v0

--- a/solution.py
+++ b/solution.py
@@ -145,7 +145,7 @@
     curvature = lax.dot_general(
         covars, loaded, contract, preferred_element_type=jnp.float32
     ) - lax.dot_general(mean_low, mean_low, contract, preferred_element_type=jnp.float32)
-    gradient, curvature = lax.psum((gradient, curvature), ("tm", "rows"))
+    gradient, curvature = lax.psum(lax.psum((gradient, curvature), "tm"), "rows")
     devices = lax.axis_size("tm") * lax.axis_size("rows")
     total = record_count * devices
     score = gradient / math.sqrt(total)

time: 1880 us -> 1950 us (1.037)
  waiting for transfers between devices: 1400 us -> 1470 us
    psum x1 -> x2, waiting for transfers between devices: 30.7 us -> 107 us  [the longest x1 71.8 us: body(): lax.psum((gradient, curvature), 'tm')]
    unnamed x7 -> x8, waiting for transfers between devices: 649 us -> 636 us
  transfers between devices with their start and end apart: 6 -> 7, of which waited for: 6 -> 7; matrix products, arithmetic and copies ran while one was open for 3% -> 2% of each run, Pallas kernels for 0% -> 0%
where the time goes in v1:
time: 1950 us
  waiting for transfers between devices  1470 us (75%)
  local copies, waits for them, and re-layouts  171 us (9%)
  blocking collectives  152 us (8%)
  other arithmetic  87.9 us (5%)
  matrix products  47.2 us (2%)
    reduce_scatter x1, waiting for transfers between devices, body(): lax.psum_scatter(cross, ('tm', 'rows'), scatter_dimension=0, tiled=True)  648 us
    unnamed x8, waiting for transfers between devices  636 us
    psum x1, waiting for transfers between devices, body(): lax.psum((gradient, curvature), 'tm')  71.8 us
    all_gather x4, blocking collectives, prefix(): pieces = jax.tree.map(lambda part: lax.all_gather(part, axis), value)  66.6 us
    psum x1, blocking collectives, body(): lax.psum((gradient, curvature), 'tm')  65.5 us
    psum x1, waiting for transfers between devices, later_moments(): shard_zero, shard_one = lax.psum((totals[0], totals[1]), 'rows')  44.5 us
  transfers between devices with their start and end apart: 7, of which 7 were waited for; matrix products, arithmetic and copies ran while one was open for 2% of the time, Pallas kernels for 0%

profile of v1, /device:TPU:0, one launch (start us, length us, event | category | flops | bytes accessed | tf_op | source)
XLA Modules:
  0.0 1948.0 jit_solution(4758874101425940531)
XLA Ops:
  8.6 23.0 %gather_fusion.3 = f32[4096]{0:T(1024)S(1)} fusion(f32[2048]{0:T(1024)S(1)} %copy-done.1, s32[4096]{0:T(1024)S(1)} %fusion.55), kind=kCustom, calls=%fused_computation.3 | custom fusion | bytes 49152 | tf_op jit(solution)/shard_map/gather | solution.py:125
  34.9 58.8 %while.105 = (s32[]{:T(128)}, f32[512]{0:T(512)S(1)}, f32[512,128]{1,0:T(8,128)S(1)}, f32[8,512]{1,0:T(8,128)S(1)}, f32[8,512,128]{2,1,0:T(8,128)}, /*index=5*/f...) while((s32[]{:T(128)}, f32[512]{0:T(512)S(1)}, ...), condition=%wide.region_1.2_spmd.clone, body=%wide.region_0.1_spmd.clone.sunk | while | flops 142807040 | bytes 2419864 | solution.py:71
  42.8 3.5 gather_fusion
  72.2 3.5 gather_fusion
  86.9 3.5 gather_fusion
  94.4 26.7 %all-gather.12.cloned.1.call-done = f32[2048,128]{1,0:T(8,128)} async-done(((f32[512,128]{1,0:T(8,128)}), f32[2048,128]{1,0:T(8,128)}) %all-gather.12.cloned.1.call-update) | async-done | bytes 1048592 | tf_op jit(solution)/shard_map/all_gather | solution.py:13
  121.9 44.5 %all-reduce.5.cloned.1.call-done = f32[1,512,128]{2,1,0:T(8,128)} async-done(((f32[1,512,128]{2,1,0:T(8,128)}), f32[1,512,128]{2,1,0:T(8,128)}) %all-reduce.5.cloned.1.call-update) | async-done | bytes 262160 | tf_op jit(solution)/shard_map/psum | solution.py:104
  166.6 9.3 psum.49
  175.9 24.5 %all-gather.3 = f32[32,1,512]{2,1,0:T(1,128)S(1)} all-gather(f32[1,1,512]{2,1,0:T(1,128)S(1)} %bitcast.202), channel_id=1, replica_groups=mesh['tm'=32,'rows'=4] {'tm'}, dimensions={0}, use_global_device_ids=true | all-gather | bytes 67584 | tf_op jit(solution)/shard_map/all_gather | solution.py:13
  200.5 10.4 all-gather.4
  212.9 9.2 all-gather.10.cloned.1.call-done
  222.1 7.5 rev.13
  229.6 33.7 %while.106 = (s32[]{:T(128)}, f32[512]{0:T(512)S(1)}, f32[512,128]{1,0:T(8,128)S(1)}, s32[]{:T(128)}, f32[32,512]{1,0:T(8,128)S(1)}, /*index=5*/f32[32,512,128]{2,1,0:T(8,128)}, s32[]{:T(128)}, s32[]{:T(128)}) while((s32[]{:T(128)}, f32[512]{0:T(512)S(1)}, f32[512,128]{1,0:T(8,128)S(1)}, s32[]{:T(128)}, f32[32,512]{1,0:T(8,128)S(1)}, ...), condition=%wide.region_5.6_spmd.clone, body=%wide.region_4.5_spmd.clone.sunk | while | flops 198148 | bytes 796787 | solution.py:25
  263.4 25.9 %gather_fusion.5 = f32[4096]{0:T(1024)S(1)} fusion(f32[512]{0:T(512)S(1)} %add.297, s32[4096]{0:T(1024)S(1)} %fusion.56), kind=kCustom, calls=%fused_computation.5 | custom fusion | bytes 49152 | tf_op jit(solution)/shard_map/gather | solution.py:131
  289.4 14.1 gather_fusion.4
  303.5 3.5 fusion.65
  307.3 65.5 %psum.51 = f32[128]{0:T(128)S(1)} all-reduce(f32[128]{0:T(128)S(1)} %fusion.53), channel_id=1, replica_groups=mesh['tm'=32,'rows'=4] {'tm'}, use_global_device_ids=true, to_apply=%region_9.10 | all-reduce | flops 128 | bytes 1024 | tf_op jit(solution)/shard_map/psum | solution.py:148
  372.8 37.0 %while.108 = (s32[]{:T(128)}, f32[512]{0:T(512)S(1)}, f32[8,512]{1,0:T(8,128)S(1)}, f32[8,512]{1,0:T(8,128)S(1)}, s32[8,512]{1,0:T(8,128)S(1)}, /*index=5*/s32[]{:T(128)}, s32[]{:T(128)}) while((s32[]{:T(128)}, f32[512]{0:T(512)S(1)}, f32[8,512]{1,0:T(8,128)S(1)}, f32[8,512]{1,0:T(8,128)S(1)}, s32[8,512]{1,0:T(8,128)S(1)}, ...), condition=%wide.region_12.13_spmd.clone, body=%wide.region_11.12_spmd.clone.sunk | while | flops 7344131 | bytes 51303 | solution.py:94
  409.8 10.4 all-reduce
  420.3 21.2 %all-gather.5 = f32[32,1,512]{2,1,0:T(1,128)S(1)} all-gather(f32[1,1,512]{2,1,0:T(1,128)S(1)} %bitcast.203), channel_id=1, replica_groups=mesh['tm'=32,'rows'=4] {'tm'}, dimensions={0}, use_global_device_ids=true | all-gather | bytes 67584 | tf_op jit(solution)/shard_map/all_gather | solution.py:13
  443.2 10.4 all-gather.6
  453.8 25.9 %gather_fusion.6 = f32[4096]{0:T(1024)S(1)} fusion(f32[512]{0:T(512)S(1)} %add.299, s32[4096]{0:T(1024)S(1)} %fusion.56), kind=kCustom, calls=%fused_computation.6 | custom fusion | bytes 49152 | tf_op jit(solution)/shard_map/gather | solution.py:137
  480.9 22.2 %scatter_custom_fusion.1 = f32[2048]{0:T(1024)S(1)} fusion(s32[4096]{0:T(1024)S(1)} %copy-done.9, f32[4096]{0:T(1024)S(1)} %get-tuple-element.904, f32[]{:T(128)} %constant.197.clone.1), kind=kCustom, calls=%fused_computation.112 | custom fusion | flops 4096 | bytes 8196 | tf_op jit(solution)/shard_map/scatter-add | solution.py:157
  503.2 6.0 fusion.52
  509.3 22.1 %scatter_custom_fusion = f32[2048]{0:T(1024)S(1)} fusion(s32[4096]{0:T(1024)S(1)} %copy-done.9, f32[4096]{0:T(1024)S(1)} %get-tuple-element.903, f32[]{:T(128)} %constant.197.clone.1), kind=kCustom, calls=%fused_computation.114 | custom fusion | flops 4096 | bytes 8196 | tf_op jit(solution)/shard_map/scatter-add | solution.py:156
  533.5 71.8 %all-reduce.7.cloned.1.call-done = f32[128,128]{0,1:T(8,128)} async-done(((f32[128,128]{0,1:T(8,128)}), f32[128,128]{0,1:T(8,128)}) %all-reduce.7.cloned.1.call-update) | async-done | bytes 65552 | tf_op jit(solution)/shard_map/psum | solution.py:148
  605.4 10.5 while.111
  605.4 5.2 fusion.107
  610.7 5.2 fusion.107
  617.5 635.7 %reduce-scatter.7.cloned.1.call-done = f32[16,2]{1,0:T(8,128)} async-done(((f32[2048,2]{1,0:T(8,128)}), f32[16,2]{1,0:T(8,128)}) %reduce-scatter.7.cloned.1.call-update) | async-done | bytes 144
  1255.3 35.4 %all-reduce.9.cloned.1.call-done = f32[128,128]{0,1:T(8,128)} async-done(((f32[128,128]{0,1:T(8,128)}), f32[128,128]{0,1:T(8,128)}) %all-reduce.9.cloned.1.call-update) | async-done | bytes 65552 | tf_op jit(solution)/shard_map/psum | solution.py:148
  1292.2 647.6 %reduce-scatter.5.cloned.1.call-done = f32[16,128]{1,0:T(8,128)} async-done(((f32[2048,128]{1,0:T(8,128)}), f32[16,128]{1,0:T(8,128)}) %reduce-scatter.5.cloned.1.call-update) | async-done | bytes 8208 | tf_op jit(solution)/shard_map/reduce_scatter | solution.py:179
  (419 shorter events, 137.7 us)
Async XLA Ops:
  7.2 24.5 %copy-start = (f32[128]{0:T(128)S(1)}, f32[128]{0:T(128)}, u32[]{:S(2)}) copy-start(f32[128]{0:T(128)} %param.26) | copy-start | bytes 1540
  7.2 1.4 copy-start.1
  7.2 114.0 %all-gather.12.cloned.1.call-start = ((), (), s32[]{:S(2)}) async-start(), calls=%async_computation.7 | async-start | bytes 1310720 | tf_op jit(solution)/shard_map/all_gather | solution.py:13
  8.6 23.1 %copy-start.2 = (bf16[4096,128]{1,0:T(8,128)(2,1)S(1)}, bf16[4096,128]{1,0:T(8,128)(2,1)}, u32[]{:S(2)}) copy-start(bf16[4096,128]{1,0:T(8,128)(2,1)} %param.21) | copy-start | bytes 3145732
  31.7 1.7 copy-start.8
  34.9 131.7 %copy-start.9 = (s32[4096]{0:T(1024)S(1)}, s32[4096]{0:T(1024)}, u32[]{:S(2)}) copy-start(s32[4096]{0:T(1024)} %param.23) | copy-start | bytes 49156
  34.9 176.2 %copy-start.7 = (s32[4096]{0:T(1024)S(1)}, s32[4096]{0:T(1024)}, u32[]{:S(2)}) copy-start(s32[4096]{0:T(1024)} %param.24) | copy-start | bytes 49156
  93.7 0.7 copy-start.3
  121.2 45.3 %all-reduce.5.cloned.1.call-start = ((), (), s32[]{:S(2)}) async-start(), calls=%async_computation.2 | async-start | bytes 524288 | tf_op jit(solution)/shard_map/psum | solution.py:104
  121.9 100.2 %all-gather.10.cloned.1.call-start = ((), (), s32[]{:S(2)}) async-start(), calls=%async_computation.3 | async-start | bytes 8650752 | tf_op jit(solution)/shard_map/all_gather | solution.py:13
  166.5 438.9 %all-reduce.7.cloned.1.call-start = ((), (), s32[]{:S(2)}) async-start(), calls=%async_computation.4 | async-start | bytes 131072 | tf_op jit(solution)/shard_map/psum | solution.py:148
  479.8 23.4 %copy-start.4 = (f32[8,512,128]{2,1,0:T(8,128)S(1)}, f32[8,512,128]{2,1,0:T(8,128)}, u32[]{:S(2)}) copy-start(f32[8,512,128]{2,1,0:T(8,128)} %get-tuple-element.649) | copy-start | bytes 6291460
  509.2 743.9 %reduce-scatter.7.cloned.1.call-start = ((), (), s32[]{:S(2)}) async-start(), calls=%async_computation.8 | async-start | bytes 1056768
  531.4 74.0 %copy-start.5 = (f32[2048,128]{1,0:T(8,128)S(1)}, f32[2048,128]{1,0:T(8,128)}, u32[]{:S(2)}) copy-start(f32[2048,128]{1,0:T(8,128)} %custom-call.9) | copy-start | bytes 3145732
  532.7 757.9 %all-reduce.9.cloned.1.call-start = ((), (), s32[]{:S(2)}) async-start(), calls=%async_computation.5 | async-start | bytes 131072 | tf_op jit(solution)/shard_map/psum | solution.py:148
  605.4 1334.5 %reduce-scatter.5.cloned.1.call-start = ((), (), s32[]{:S(2)}) async-start(), calls=%async_computation.6 | async-start | bytes 1056768 | tf_op jit(solution)/shard_map/reduce_scatter | solution.py:179
  616.0 1.0 copy-start.6
Sparse Core Ops, SparseCore 0:
  94.6 26.5 all-gather.11
  124.3 42.1 all-reduce.4
  168.7 53.3 all-gather.9
  509.4 95.9 all-reduce.6
  607.5 645.5 reduce-scatter.6
  1255.3 35.2 all-reduce.8
  1293.0 646.8 reduce-scatter.4
